TPU v7x, 32 devices: a whole 2x2x4 slice. The times are simulated.
32 devices in a mesh: grp: 4 (over z), seq: 8 (over y, x, core).
Axes of the slice: x: 2, y: 2, z: 4, core: 2. Of those that a mesh axis runs over, the one named last changes fastest.
Arguments:
- tokens: bfloat16 [128, 256, 768], P(('grp', 'seq')), may hold values from -6 to 6
- cotangent: bfloat16 [128, 256, 768], P(('grp', 'seq')), may hold values from -6 to 6
- frame_clip: int32 [128], P('grp'), may hold values from 0 to 15, as said below
- frame_valid: int32 [128], P('grp'), may hold values from 0 to 1, as said below
- place_valid: int32 [16, 256], P('grp'), may hold values from 0 to 1, as said below
- time_gain: float32 [768], P('seq'), may hold values from 0.5 to 1.5
- time_shift: float32 [768], P('seq'), may hold values from -1.75 to 1.75
- time_inward: float32 [768, 2304], P('grp', 'seq'), may hold values from -0.21875 to 0.21875
- time_inward_bias: float32 [1536], P('seq'), may hold values from -1.75 to 1.75
- time_outward: float32 [768, 768], P('grp', 'seq'), may hold values from -0.3125 to 0.3125
- time_outward_bias: float32 [768], P('seq'), may hold values from -1.75 to 1.75
- time_linear: float32 [768, 768], P('grp', 'seq'), may hold values from -0.21875 to 0.21875
- time_linear_bias: float32 [768], P('seq'), may hold values from -1.75 to 1.75
- space_gain: float32 [768], P('seq'), may hold values from 0.5 to 1.5
- space_shift: float32 [768], P('seq'), may hold values from -1.75 to 1.75
- space_inward: float32 [768, 2304], P('grp', 'seq'), may hold values from -0.21875 to 0.21875
- space_inward_bias: float32 [1536], P('seq'), may hold values from -1.75 to 1.75
- space_outward: float32 [768, 768], P('grp', 'seq'), may hold values from -0.875 to 0.875
- space_outward_bias: float32 [768], P('seq'), may hold values from -1.75 to 1.75
- feed_gain: float32 [768], P('seq'), may hold values from 0.5 to 1.5
- feed_shift: float32 [768], P('seq'), may hold values from -1.75 to 1.75
- feed_expand: float32 [768, 3072], P('grp', 'seq'), may hold values from -0.21875 to 0.21875
- feed_expand_bias: float32 [3072], P('seq'), may hold values from -1.75 to 1.75
- feed_reduce: float32 [3072, 768], P('grp', 'seq'), may hold values from -0.15625 to 0.15625
- feed_reduce_bias: float32 [768], P('seq'), may hold values from -1.75 to 1.75
Outputs:
- result: bfloat16 [128, 256, 768], P(('grp', 'seq'))
- input_gradient: float32 [128, 256, 768], P(('grp', 'seq'))
- gradient_time_gain: float32 [768], P('seq')
- gradient_time_shift: float32 [768], P('seq')
- gradient_time_inward: float32 [768, 2304], P('grp', 'seq')
- gradient_time_inward_bias: float32 [1536], P('seq')
- gradient_time_outward: float32 [768, 768], P('grp', 'seq')
- gradient_time_outward_bias: float32 [768], P('seq')
- gradient_time_linear: float32 [768, 768], P('grp', 'seq')
- gradient_time_linear_bias: float32 [768], P('seq')
- gradient_space_gain: float32 [768], P('seq')
- gradient_space_shift: float32 [768], P('seq')
- gradient_space_inward: float32 [768, 2304], P('grp', 'seq')
- gradient_space_inward_bias: float32 [1536], P('seq')
- gradient_space_outward: float32 [768, 768], P('grp', 'seq')
- gradient_space_outward_bias: float32 [768], P('seq')
- gradient_feed_gain: float32 [768], P('seq')
- gradient_feed_shift: float32 [768], P('seq')
- gradient_feed_expand: float32 [768, 3072], P('grp', 'seq')
- gradient_feed_expand_bias: float32 [3072], P('seq')
- gradient_feed_reduce: float32 [3072, 768], P('grp', 'seq')
- gradient_feed_reduce_bias: float32 [768], P('seq')
Inputs may be any that keep to these rules, and one draw needn't show every extreme that they name: `frame_clip`: the g-th run of 32 consecutive frames belongs to the clips g * 4 to g * 4 + 3, each clip having exactly 8 of these frames, in any order. `frame_valid`: every clip has at least 4 valid frames. `place_valid`: in every clip the valid places are the first ones, at least 128 of them.
All inputs are finite; a program needn't handle non-finite values.
Results may differ from a plain program's by a relative error of at most 0.02.
Values may be sent and summed in bfloat16 or wider, within the bound.
A program may use at most 256 MiB of HBM per device.

v0:
```python
import jax
import jax.numpy as jnp
from jax import lax
from jax.experimental import pallas as pl
from jax.experimental.pallas import tpu as pltpu
from jax.sharding import PartitionSpec as P

MESH = pl.DeviceIdType.MESH
BF = jnp.bfloat16
F32 = jnp.float32
NN = (((1,), (0,)), ((), ()))
NT = (((1,), (1,)), ((), ()))
TN = (((0,), (0,)), ((), ()))

TI, TO, TL, SI, SO, FE, FR = 0, 2304, 3072, 3840, 6144, 6912, 9984
WROWS = 13056
BASE = ([96 * t for t in range(3)] + [TO, TL] + [SI + 96 * t for t in range(3)] + [SO]
        + [FE + 768 * (v // 2) + 96 * (v % 2) for v in range(4)] + [FR + 768 * t for t in range(4)])
PAIR = [576] * 3 + [192] * 2 + [576] * 3 + [192] + [192] * 4 + [192] * 4
CORE = [288] * 3 + [96] * 2 + [288] * 3 + [96] + [1536] * 4 + [96] * 4
CHUNKS = 17
GATHER_ORDER = [0, 1, 2, 3, 4, 5, 6, 7, 8, 9, 10, 13, 15, 11, 12, 14, 16]
SLOTS = 5
LAGS = (1, 2, 2, 2)
GATHER_LAGS = (1, 2, 1)
SPACING = 2
KINDS = ("p", "q", "so", "d", "sp", "sq", "sd")
EPSILON = 1e-06


def dot(a, b, dims):
    return lax.dot_general(a, b, dims, preferred_element_type=F32)


class Links:
    def __init__(self, send_sem, recv_sem):
        self.send_sem, self.recv_sem = send_sem, recv_sem
        self.copies, self.used, self.sent = {}, 0, set()
        self.z = lax.axis_index("grp")
        s = self.s = lax.axis_index("seq")
        core, x, y = s % 2, (s // 2) % 2, s // 4
        xn, yn = s + 2 - 4 * x, s + 4 - 8 * y
        self.core = core
        self.sib = s + 1 - 2 * core
        self.p = yn * (1 - core) + xn * core
        self.q = xn * (1 - core) + yn * core
        self.d = xn + yn - s

    def zpeer(self, k):
        return (self.z + k) % 4

    def speer(self, k):
        return (self.s + k) % 8

    def greet(self):
        bar = pltpu.get_barrier_semaphore()
        for k in range(1, 8):
            pl.semaphore_signal(bar, inc=1, device_id=(self.z, self.speer(k)), device_id_type=MESH)
        for k in range(1, 4):
            pl.semaphore_signal(bar, inc=1, device_id=(self.zpeer(k), self.s), device_id_type=MESH)

    def greeted(self):
        pl.semaphore_wait(pltpu.get_barrier_semaphore(), 10)

    def send(self, key, src, dst, device):
        i = self.used
        self.used += 1
        copy = pltpu.make_async_remote_copy(
            src_ref=src, dst_ref=dst, send_sem=self.send_sem.at[i], recv_sem=self.recv_sem.at[i],
            device_id=device, device_id_type=MESH)
        copy.start()
        self.copies[key] = copy

    def sends(self, key, src, dst, seq):
        self.send(key, src, dst, (self.z, seq))

    def sendz(self, key, src, dst, z):
        self.send(key, src, dst, (z, self.s))

    def got(self, *keys):
        for key in keys:
            self.copies[key].wait_recv()

    def gone(self, *keys):
        for key in keys:
            if key not in self.sent:
                self.sent.add(key)
                self.copies[key].wait_send()

    def drain(self):
        self.gone(*self.copies)


class Local:
    def __init__(self, sem):
        self.sem, self.used, self.copies = sem, 0, {}

    def start(self, key, src, dst):
        copy = pltpu.make_async_copy(src, dst, self.sem.at[self.used])
        self.used += 1
        copy.start()
        self.copies[key] = copy

    def wait(self, *keys):
        for key in keys:
            copy = self.copies.pop(key, None)
            if copy is not None:
                copy.wait()

    def drain(self):
        self.wait(*list(self.copies))


def place(c, s):
    return pl.ds(pl.multiple_of(BASE[c] + PAIR[c] * (s // 2) + CORE[c] * (s % 2), 32), 96)


def block(ref, c, s):
    return ref.at[place(c, s)]


class Gather:
    def __init__(self, links, zst, w):
        self.l, self.zst, self.w = links, zst, w
        self.next, self.flight, self.zsent, self.clock = 0, [], 0, 0

    def zsend(self, count=1):
        for i in range(self.zsent, min(self.zsent + count, CHUNKS)):
            c = GATHER_ORDER[i]
            own = self.zst.at[self.l.z, c]
            for k in range(1, 4):
                self.l.sendz(("zg", c, k), own, own, self.l.zpeer(k))
            self.zsent += 1

    def sources(self, *chunks):
        self.l.gone(*[(k, c) for c in chunks for k in KINDS])

    def step_a(self, i, c):
        l = self.l
        l.got(*[("zg", c, k) for k in range(1, 4)])
        rows = place(c, l.s)
        zst, w = self.zst, self.w
        for half in range(2):
            lo, hi = zst[2 * half, c], zst[2 * half + 1, c]
            w[rows, 384 * half:384 * half + 128] = lo[:96]
            w[rows, 384 * half + 256:384 * half + 384] = hi[:96]
            blo, bhi = lo[96:], hi[96:]
            w[rows, 384 * half + 128:384 * half + 256] = jnp.concatenate([
                jnp.concatenate([blo[:, :64], bhi[:, :64]], axis=1),
                jnp.concatenate([blo[:, 64:], bhi[:, 64:]], axis=1)], axis=0)
        own = block(w, c, l.s)
        l.sends(("p", c), own, own, l.p)
        l.sends(("q", c), own, own, l.q)
        l.sends(("so", c), own, own, l.sib)
        self.zsend()

    def step_b(self, i, c):
        l = self.l
        l.got(("p", c))
        bp = block(self.w, c, l.p)
        l.sends(("d", c), bp, bp, l.q)
        l.sends(("sp", c), bp, bp, l.sib)
        l.got(("q", c))
        bq = block(self.w, c, l.q)
        l.sends(("sq", c), bq, bq, l.sib)

    def step_c(self, i, c):
        l = self.l
        l.got(("d", c))
        bd = block(self.w, c, l.d)
        l.sends(("sd", c), bd, bd, l.sib)

    def step_d(self, i, c):
        self.l.got(("so", c), ("sp", c), ("sq", c), ("sd", c))

    def tick(self, push=True, whole=-1):
        steps = (self.step_b, self.step_c, self.step_d)
        self.clock += 1
        fresh = []
        if push and self.next < CHUNKS:
            self.step_a(self.next, GATHER_ORDER[self.next])
            fresh = [(self.next, 0, self.clock + GATHER_LAGS[0])]
            self.next += 1
        later = []
        for i, k, due in self.flight:
            if i <= whole or self.clock >= due:
                steps[k](i, GATHER_ORDER[i])
                k, due = k + 1, self.clock + (GATHER_LAGS + (0,))[k + 1]
            if k < 3:
                later.append((i, k, due))
        self.flight = later + fresh

    def until(self, chunk):
        i = GATHER_ORDER.index(chunk)
        while i >= self.next or any(j <= i for j, _, _ in self.flight):
            self.tick(push=self.next <= i, whole=i)

    @property
    def done(self):
        return self.next == CHUNKS and not self.flight


class Scatter:
    def __init__(self, links, g, sr, fr, ar, br, zp, zr, write):
        self.l, self.g, self.sr, self.fr, self.ar, self.br = links, g, sr, fr, ar, br
        self.zp, self.zr, self.write = zp, zr, write
        self.ready, self.flight, self.order = [], [], []
        self.clock, self.pushed = 0, -9

    def step_a(self, i, c):
        l = self.l
        for j in range(4):
            l.sends(("s", c, j), block(self.g, c, 2 * j + 1 - l.core), self.sr.at[i % SLOTS, j], l.sib)

    def add(self, c, s, other):
        rows = place(c, s)
        self.g[rows, :] = (self.g[rows, :].astype(F32) + other.astype(F32)).astype(BF)

    def step_b(self, i, c):
        l, k = self.l, i % SLOTS
        l.got(*[("s", c, j) for j in range(4)])
        for s, j in ((l.d, l.d // 2), (l.p, l.p // 2), (l.q, l.q // 2), (l.s, l.s // 2)):
            self.add(c, s, self.sr[k, j])
            if s is l.d:
                l.sends(("f", c), block(self.g, c, l.d), self.fr.at[k], l.p)
            if s is l.p:
                l.sends(("a", c), block(self.g, c, l.p), self.ar.at[k], l.p)

    def step_c(self, i, c):
        l, k = self.l, i % SLOTS
        l.got(("f", c))
        self.add(c, l.q, self.fr[k])
        l.sends(("b", c), block(self.g, c, l.q), self.br.at[k], l.q)

    def step_d(self, i, c):
        l, k = self.l, i % SLOTS
        l.got(("a", c), ("b", c))
        rows = place(c, l.s)
        total = self.g[rows, :].astype(F32) + self.ar[k].astype(F32) + self.br[k].astype(F32)
        if i >= SLOTS:
            l.gone(*[("z", self.order[i - SLOTS], j) for j in range(1, 4)])
        zp = self.zp
        for half in range(2):
            lane = 384 * half
            zp[k, 2 * half, 0:96] = total[:, lane:lane + 128].astype(BF)
            zp[k, 2 * half + 1, 0:96] = total[:, lane + 256:lane + 384].astype(BF)
            mid = total[:, lane + 128:lane + 256]
            top, low = mid[:48], mid[48:]
            zp[k, 2 * half, 96:144] = jnp.concatenate([top[:, :64], low[:, :64]], axis=1).astype(BF)
            zp[k, 2 * half + 1, 96:144] = jnp.concatenate([top[:, 64:], low[:, 64:]], axis=1).astype(BF)
        for j in range(1, 4):
            z = l.zpeer(j)
            l.sendz(("z", c, j), zp.at[k, z], self.zr.at[k, j - 1], z)

    def step_e(self, i, c):
        l, k = self.l, i % SLOTS
        l.got(*[("z", c, j) for j in range(1, 4)])
        total = self.zp[k, l.z].astype(F32)
        for j in range(3):
            total += self.zr[k, j].astype(F32)
        self.write(c, total)

    def pump(self, rush=False):
        steps = (self.step_b, self.step_c, self.step_d, self.step_e)
        self.clock += 1
        fresh = []
        if self.ready and (rush or self.clock >= self.pushed + SPACING):
            c = self.ready.pop(0)
            i = len(self.order)
            self.order.append(c)
            self.step_a(i, c)
            self.pushed = self.clock
            fresh = [(i, 0, self.clock + LAGS[0])]
        later = []
        for i, k, due in self.flight:
            if rush or self.clock >= due:
                steps[k](i, self.order[i])
                k, due = k + 1, self.clock + (LAGS + (0,))[k + 1]
            if k < 4:
                later.append((i, k, due))
        self.flight = later + fresh

    def finish(self):
        while self.ready or self.flight:
            self.pump(rush=True)


class VectorSum:
    def __init__(self, links, gv, vb):
        self.l, self.gv, self.vb = links, gv, vb

    def swap(self, i):
        l = self.l
        l.sends(("vs", i), self.gv.at[i], self.vb.at[i], (l.sib, l.p, l.q)[i])

    def join(self, i):
        self.l.got(("vs", i))
        self.gv[i + 1] = self.gv[i] + self.vb[i]

    def swapz(self):
        l = self.l
        self.vb[3 + l.z] = self.gv[3]
        for k in range(1, 4):
            l.sendz(("vz", k), self.gv.at[3], self.vb.at[3 + l.z], l.zpeer(k))

    def total(self):
        self.l.got(*[("vz", k) for k in range(1, 4)])
        return (self.vb[3] + self.vb[4]) + (self.vb[5] + self.vb[6])


TG, TS, TOB, TLB, SG, SS, SOB, FG, FS, FRB, TIB, SIB, FEB = 0, 1, 2, 3, 4, 5, 6, 7, 8, 9, 10, 12, 14


def assemble_vectors(vg, vec):
    vec[...] = jnp.zeros(vec.shape, F32)
    for s in range(8):
        piece = vg[s]
        vec[0:10, 96 * s:96 * s + 96] = piece[0:10, 0:96]
        for a in range(2):
            i = 2 * s + a
            for r in (TIB, SIB):
                vec[r + i // 8:r + i // 8 + 1, 96 * (i % 8):96 * (i % 8) + 96] = piece[r + a:r + a + 1, 0:96]
        for a in range(4):
            t, lane = 2 * (s % 2) + a // 2, 192 * (s // 2) + 96 * (a % 2)
            vec[FEB + t:FEB + 1 + t, lane:lane + 96] = piece[FEB + a:FEB + 1 + a, 0:96]


def selectors(odd, ea, el, eh, eb):
    m = lax.broadcasted_iota(jnp.int32, (192, 128), 0)
    c = lax.broadcasted_iota(jnp.int32, (192, 128), 1)
    whole, folded = c + 64 * odd, c % 64 + 128 * (1 - odd)
    ea[...] = jnp.where(m == whole, 1.0, 0.0).astype(BF)
    both = jnp.where(m == folded, 1.0, 0.0)
    el[...] = jnp.where(c < 64, both, 0.0).astype(BF)
    eh[...] = jnp.where(c < 64, 0.0, both).astype(BF)
    eb[...] = both.astype(BF)


def standardize(x):
    centered = x - jnp.mean(x, axis=-1, keepdims=True)
    scale = lax.rsqrt(jnp.mean(centered * centered, axis=-1, keepdims=True) + EPSILON)
    return centered * scale, scale


def norm_back(e, gain, n, scale):
    u = e * gain
    return scale * (u - jnp.mean(u, axis=-1, keepdims=True) - n * jnp.mean(u * n, axis=-1, keepdims=True))


def column_sums(x):
    return jnp.sum(x, axis=0, keepdims=True)


def head_masks(scale):
    lane = lax.broadcasted_iota(jnp.int32, (1, 128), 1)
    return [jnp.where(lane < 64, scale, 0.0).astype(BF), jnp.where(lane < 64, 0.0, scale).astype(BF)]


def pair_columns(qkv, rows, p):
    c = pl.multiple_of(p * 128, 128)
    return [qkv[rows, pl.ds(768 * j + c, 128)] for j in range(3)]


def attend_block(b, qkv, mixed, lse, bias):
    rows = pl.ds(b * 256, 256)

    def pair(p):
        q, k, v = pair_columns(qkv, rows, p)
        scaled, plain = head_masks(0.125), head_masks(1.0)
        out = None
        for h in range(2):
            s = dot(k * scaled[h], q, NT) + bias()
            m = jnp.max(s, axis=0, keepdims=True)
            e = jnp.exp(s - m)
            total = jnp.sum(e, axis=0, keepdims=True)
            lse[pl.ds(b * 12 + p * 2 + h, 1), :] = m + jnp.log(total)
            o = dot((e * (1.0 / total)).astype(BF), v * plain[h], TN)
            out = o if out is None else out + o
        mixed[rows, pl.ds(pl.multiple_of(p * 128, 128), 128)] = out.astype(BF)

    def body(i, _):
        pair(2 * i)
        pair(2 * i + 1)
        return 0

    lax.fori_loop(0, 3, body, 0)


def attend_block_back(b, qkv, gm, lse, bias):
    rows = pl.ds(b * 256, 256)

    def pair(p):
        q, k, v = pair_columns(qkv, rows, p)
        c = pl.multiple_of(p * 128, 128)
        g = gm[rows, pl.ds(c, 128)]
        scaled, plain = head_masks(0.125), head_masks(1.0)
        sums = [None, None, None]
        for h in range(2):
            kh, vh, qh, gh = k * scaled[h], v * plain[h], q * scaled[h], g * plain[h]
            s = dot(kh, q, NT) + bias()
            chances = jnp.exp(s - lse[pl.ds(b * 12 + p * 2 + h, 1), :])
            back = dot(vh, g, NT)
            mean = jnp.sum(chances * back, axis=0, keepdims=True)
            gs = (chances * (back - mean)).astype(BF)
            for j, term in enumerate((dot(gs, kh, TN), dot(gs, qh, NN), dot(chances.astype(BF), gh, NN))):
                sums[j] = term if sums[j] is None else sums[j] + term
        for j in range(3):
            qkv[rows, pl.ds(768 * j + c, 128)] = sums[j].astype(BF)

    def body(i, _):
        pair(2 * i)
        pair(2 * i + 1)
        return 0

    lax.fori_loop(0, 3, body, 0)


def project_in(normed, w, at, qkv, rows, vec, bias_row):
    for j in range(3):
        part = dot(normed, w[at + 768 * j:at + 768 * (j + 1), :], NT)
        if j != 1:
            r = bias_row + j // 2
            part = part + vec[r:r + 1, :]
        qkv[rows, 768 * j:768 * (j + 1)] = part.astype(BF)


def weight_gradient(out, delta, column, rows):
    for m in range(3):
        lane = column + 256 * m
        out[256 * m:256 * m + 256, :] = dot(delta[:, lane:lane + 256], rows[...], TN).astype(BF)


def flat(x):
    return x.astype(F32).reshape(256, 768)


def tiled(x):
    return x.reshape(32, 8, 768).astype(BF)


def layer_kernel(
    tokens, cot_i, clip_i, valid_i, place_i, vin, ti_i, to_i, tl_i, si_i, so_i, fe_i, fr_i,
    result_o, grad_o, tg_o, ts_o, gti, tib_o, gto, tob_o, gtl, tlb_o, sg_o, ss_o, gsi, sib_o, gso, sob_o, fg_o, fs_o, gfe, feb_o,
    gfr, frb_o, tqkv_o, tmixed_o, ret_o, first_o, xp_o,
    w, zst, vg, vec, ea, el, eh, eb, tmask, smask, frames_a, frames_b, places_a, places_b, nb, mixed, qkv, f1, f2, f3, act, gh, g,
    sr, fr, ar, br, zp, zr, gv, vb, lse, local_sem, send_sem, recv_sem,
):
    l = Links(send_sem, recv_sem)
    l.greet()
    here = Local(local_sem)
    mine = pl.ds(4 * l.s, 4)
    xp, gpp = places_a, places_a
    pr, gb = places_b, places_b
    ret, it = frames_a, frames_a
    x, gp = frames_b, frames_b
    here.start("x", tokens, x)
    here.start("xp", tokens.at[:, mine], xp.at[mine])
    here.start("cot", cot_i, g)
    odd = l.z % 2
    selectors(odd, ea, el, eh, eb)
    ga = Gather(l, zst, w)

    def pack(ref, chunks):
        low = ref[...].astype(BF)
        a, bl, bh = dot(low, ea[...], TN), dot(low, el[...], TN), dot(low, eh[...], TN)
        for t, c in enumerate(chunks):
            zst[l.z, c, 0:96] = a[96 * t:96 * t + 96].astype(BF)
            zst[l.z, c, 96:144] = (bl[96 * t:96 * t + 48] + bh[96 * t + 48:96 * t + 96]).astype(BF)

    def masks():
        clips, flags = clip_i[...].astype(F32), valid_i[...].astype(F32)
        row32 = lax.broadcasted_iota(jnp.int32, (256, 32), 0) // 8
        spread = jnp.where(row32 == lax.broadcasted_iota(jnp.int32, (256, 32), 1), 1.0, 0.0)
        clip_key = jnp.sum(spread * clips, axis=1, keepdims=True)
        flag_key = jnp.sum(spread * flags, axis=1, keepdims=True)
        clip_query = dot(jnp.broadcast_to(clips, (8, 32)).astype(BF), spread.astype(BF), NT)[0:1]
        j = lax.broadcasted_iota(jnp.int32, (256, 256), 0)
        i = lax.broadcasted_iota(jnp.int32, (256, 256), 1)
        allowed = (clip_key == clip_query) & (flag_key > 0.5) & (j % 8 == i % 8)
        tmask[...] = jnp.where(allowed, 0.0, -1e30)
        clip_row = lax.broadcasted_iota(jnp.int32, (4, 32), 0)
        which = jnp.where((clip_i[...] % 4) == clip_row, 1.0, 0.0)
        frame_of = lax.broadcasted_iota(jnp.int32, (32, 128), 0)
        own = jnp.where(frame_of == lax.broadcasted_iota(jnp.int32, (32, 128), 1) + 4 * l.s, 1.0, 0.0)
        chosen = dot(which.astype(BF), own.astype(BF), NN)
        open_places = dot(place_i[...].astype(F32).astype(BF), chosen.astype(BF), TN)
        for f in range(4):
            smask[f] = jnp.where(open_places[:, f:f + 1] > 0.5, 0.0, -1e30)

    pack(ti_i, [0, 1, 2])
    vg[l.s] = vin[...].astype(BF).astype(F32)
    l.greeted()
    ga.zsend(3)
    for k in range(1, 8):
        peer = l.speer(k)
        l.sends(("t", k), tokens.at[:, pl.ds(4 * peer, 4)], xp.at[mine], peer)
        l.sends(("v", k), vg.at[l.s], vg.at[l.s], peer)
    pack(to_i, [3])
    pack(tl_i, [4])
    ga.tick()
    pack(si_i, [5, 6, 7])
    ga.tick()
    pack(so_i, [8])
    pack(fe_i, [9, 10, 11, 12])
    ga.tick()
    ga.zsend(2)
    for t in range(4):
        pack(fr_i.at[192 * t:192 * t + 192], [13 + t])
    ga.tick()
    masks()
    l.got(*[("v", k) for k in range(1, 8)])
    assemble_vectors(vg, vec)
    l.got(*[("t", k) for k in range(1, 8)])
    here.wait("x", "xp")
    here.start("xp_o", xp, xp_o)
    for b in range(4):
        rows = pl.ds(b * 256, 256)
        n, _ = standardize(flat(xp[:, b]))
        nb[rows, :] = (n * vec[TG:TG + 1, :] + vec[TS:TS + 1, :]).astype(BF)
    ga.until(2)
    for b in range(4):
        project_in(nb[256 * b:256 * b + 256, :], w, TI, qkv, pl.ds(b * 256, 256), vec, TIB)
        if b % 2:
            ga.tick()
    here.start("tqkv_o", qkv, tqkv_o)
    here.wait("xp_o")
    ga.until(3)
    for b in range(4):
        attend_block(b, qkv, mixed, lse.at[0:48], lambda: tmask[...])
        o = dot(mixed[256 * b:256 * b + 256, :], w[TO:TO + 768, :], NT) + vec[TOB:TOB + 1, :]
        pr[:, b] = tiled(o)
        ret[:, 4 * l.s + b] = pr[mine, b]
        for k in range(1, 8):
            peer = l.speer(k)
            l.sends(("r", b, k), pr.at[pl.ds(4 * peer, 4), b], ret.at[:, 4 * l.s + b], peer)
        ga.tick()
    here.start("tmixed_o", mixed, tmixed_o)
    ga.until(4)
    for b in range(4):
        l.got(*[("r", b, k) for k in range(1, 8)])
    first = second = f1
    for f in range(4):
        rows = pl.ds(256 * f, 256)
        back = flat(ret[f]).astype(BF)
        gh[rows, :] = back
        total = flat(x[f]) + dot(back, w[TL:TL + 768, :], NT) + vec[TLB:TLB + 1, :]
        first[rows, :] = total
        n, _ = standardize(total)
        nb[rows, :] = (n * vec[SG:SG + 1, :] + vec[SS:SS + 1, :]).astype(BF)
        if f == 1:
            ga.tick()
    here.start("ret_o", gh, ret_o)
    here.start("first_o", first, first_o)
    ga.until(7)
    here.wait("tqkv_o", "tmixed_o")
    for f in range(4):
        rows = pl.ds(256 * f, 256)
        project_in(nb[256 * f:256 * f + 256, :], w, SI, qkv, rows, vec, SIB)
        attend_block(f, qkv, mixed, lse.at[48:96], lambda: smask[f])
        ga.tick()
    ga.until(8)
    here.wait("first_o", "ret_o", "cot")

    final, dfn = f2, f3
    for f in range(4):
        rows = pl.ds(256 * f, 256)
        value = first[rows, :] + dot(mixed[rows, :], w[SO:SO + 768, :], NT) + vec[SOB:SOB + 1, :]
        second[rows, :] = value
        n, _ = standardize(value)
        nb[rows, :] = (n * vec[FG:FG + 1, :] + vec[FS:FS + 1, :]).astype(BF)
        final[rows, :] = value + vec[FRB:FRB + 1, :]
        dfn[rows, :] = jnp.zeros((256, 768), F32)

    into = {0: gti, 1: gti, 2: gti, 3: gto, 4: gtl, 5: gsi, 6: gsi, 7: gsi, 8: gso, 9: gfe, 10: gfe, 11: gfe, 12: gfe}

    def write(c, total):
        a, folded = total[:96], total[96:]
        lane = lax.broadcasted_iota(jnp.int32, (48, 128), 1)
        b = jnp.concatenate([jnp.where(lane < 64, folded, 0.0), jnp.where(lane < 64, 0.0, folded)], axis=0)
        a_high, b_high = a.astype(BF), b.astype(BF)
        a_low, b_low = (a - a_high.astype(F32)).astype(BF), (b - b_high.astype(F32)).astype(BF)
        value = (dot(ea[...], a_high, NT) + dot(eb[...], b_high, NT)) + (dot(ea[...], a_low, NT) + dot(eb[...], b_low, NT))
        if c >= 13:
            gfr[192 * (c - 13):192 * (c - 12), :] = value
        else:
            t = c - [k for k in into if into[k] is into[c]][0]
            into[c][:, 96 * t:96 * t + 96] = value

    sc = Scatter(l, w, sr, fr, ar, br, zp, zr, write)
    vs = VectorSum(l, gv, vb)
    sums = gv.at[0]
    sums[...] = jnp.zeros((24, 768), F32)

    def note(r, value):
        sums[r:r + 1, :] += value

    def pump():
        if not ga.done:
            ga.tick()
        sc.pump()

    for step, t in enumerate((0, 2, 1, 3)):
        ga.until(10 if t % 2 == 0 else 12)
        ga.until(13 + t)
        we, wf = w.at[FE + 768 * t:FE + 768 * (t + 1)], w.at[FR + 768 * t:FR + 768 * (t + 1)]

        def unit(b, _):
            rows = pl.ds(pl.multiple_of(256 * b, 256), 256)
            u = dot(nb[rows, :], we[...], NT) + vec[FEB + t:FEB + t + 1, :]
            phi = 0.5 + 0.5 * lax.erf(u * 0.7071067811865476)
            a = (u * phi).astype(BF)
            act[rows, :] = a
            slope = phi + u * (0.3989422804014327 * jnp.exp(-0.5 * u * u))
            h = (dot(g[rows, :], wf[...], NN) * slope).astype(BF)
            gh[rows, :] = h
            final[rows, :] += dot(a, wf[...], NT)
            dfn[rows, :] += dot(h, we[...], NN)
            sums[FEB + t:FEB + t + 1, :] += column_sums(h.astype(F32))
            return 0

        lax.fori_loop(0, 2, unit, 0)
        pump()
        lax.fori_loop(2, 4, unit, 0)
        pump()
        ga.sources(13 + t)
        weight_gradient(wf, g, 0, act)
        sc.ready.append(13 + t)
        pump()
        ga.sources(*((9, 10) if t % 2 == 0 else (11, 12)))
        weight_gradient(we, gh, 0, nb)
        if step % 2:
            sc.ready += [9, 10] if step == 1 else [11, 12]
        pump()

    ga.sources(*GATHER_ORDER)
    for f in range(4):
        rows = pl.ds(256 * f, 256)
        nb[rows, :] = final[rows, :].astype(BF)
        n, scale = standardize(second[rows, :])
        e = dfn[rows, :]
        cot = g[rows, :].astype(F32)
        note(FRB, column_sums(cot))
        note(FG, column_sums(e * n))
        note(FS, column_sums(e))
        total = cot + norm_back(e, vec[FG:FG + 1, :], n, scale)
        final[rows, :] = total
        low = total.astype(BF)
        act[rows, :] = low
        note(SOB, column_sums(low.astype(F32)))
        gh[rows, :] = dot(low, w[SO:SO + 768, :], NN).astype(BF)
        if f % 2:
            sc.pump(rush=True)
    here.start("result", nb, result_o)
    here.start("first", first_o, first)
    weight_gradient(w.at[SO:SO + 768], act, 0, mixed)
    here.start("mixed2", tmixed_o, mixed)
    sc.ready.append(8)
    sc.pump(rush=True)
    l.gone(*[("r", b, k) for b in range(4) for k in range(1, 8)])
    here.start("xp2", xp_o, places_b)
    here.wait("result", "first")
    for f in range(4):
        rows = pl.ds(256 * f, 256)
        attend_block_back(f, qkv, gh, lse.at[48:96], lambda: smask[f])
        n, scale = standardize(first[rows, :])
        nb[rows, :] = (n * vec[SG:SG + 1, :] + vec[SS:SS + 1, :]).astype(BF)
        joined = qkv[rows, :]
        note(SIB, column_sums(joined[:, :768].astype(F32)))
        note(SIB + 1, column_sums(joined[:, 1536:].astype(F32)))
        e = dot(joined, w[SI:SI + 2304, :], NN)
        note(SG, column_sums(e * n))
        note(SS, column_sums(e))
        total = final[rows, :] + norm_back(e, vec[SG:SG + 1, :], n, scale)
        final[rows, :] = total
        low = total.astype(BF)
        act[rows, :] = low
        note(TLB, column_sums(low.astype(F32)))
        gp[f] = tiled(dot(low, w[TL:TL + 768, :], NN))
        gpp[4 * l.s + f] = gp[f, pl.ds(4 * l.s, 4)]
        for k in range(1, 8):
            peer = l.speer(k)
            l.sends(("g", f, k), gp.at[f, pl.ds(4 * peer, 4)], gpp.at[4 * l.s + f], peer)
        sc.pump(rush=True)
    here.start("ret", ret_o, gh)
    for j in range(3):
        weight_gradient(w.at[SI + 768 * j:SI + 768 * (j + 1)], qkv, 768 * j, nb)
    here.start("qkv2", tqkv_o, qkv)
    sc.ready += [5, 6, 7]
    sc.pump(rush=True)
    here.wait("ret")
    weight_gradient(w.at[TL:TL + 768], act, 0, gh)
    sc.ready.append(4)
    sc.pump(rush=True)

    for f in range(4):
        l.got(*[("g", f, k) for k in range(1, 8)])
    for b in range(4):
        rows = pl.ds(256 * b, 256)
        low = flat(gpp[:, b])
        note(TOB, column_sums(low))
        low = low.astype(BF)
        act[rows, :] = low
        gh[rows, :] = dot(low, w[TO:TO + 768, :], NN).astype(BF)
    sc.pump(rush=True)
    here.wait("mixed2")
    weight_gradient(w.at[TO:TO + 768], act, 0, mixed)
    sc.ready.append(3)
    sc.pump(rush=True)
    here.wait("qkv2", "xp2")
    for b in range(4):
        rows = pl.ds(256 * b, 256)
        attend_block_back(b, qkv, gh, lse.at[0:48], lambda: tmask[...])
        n, scale = standardize(flat(places_b[:, b]))
        nb[rows, :] = (n * vec[TG:TG + 1, :] + vec[TS:TS + 1, :]).astype(BF)
        joined = qkv[rows, :]
        note(TIB, column_sums(joined[:, :768].astype(F32)))
        note(TIB + 1, column_sums(joined[:, 1536:].astype(F32)))
        e = dot(joined, w[TI:TI + 2304, :], NN)
        note(TG, column_sums(e * n))
        note(TS, column_sums(e))
        gb[:, b] = tiled(norm_back(e, vec[TG:TG + 1, :], n, scale))
        it[:, 4 * l.s + b] = gb[mine, b]
        for k in range(1, 8):
            peer = l.speer(k)
            l.sends(("h", b, k), gb.at[pl.ds(4 * peer, 4), b], it.at[:, 4 * l.s + b], peer)
        sc.pump(rush=True)
    for j in range(3):
        weight_gradient(w.at[TI + 768 * j:TI + 768 * (j + 1)], qkv, 768 * j, nb)
    sc.ready += [0, 1, 2]
    for i in range(3):
        vs.swap(i)
        sc.pump(rush=True)
        vs.join(i)
    vs.swapz()
    for b in range(4):
        l.got(*[("h", b, k) for k in range(1, 8)])
    for f in range(4):
        rows = pl.ds(256 * f, 256)
        final[rows, :] += flat(it[f])
    here.start("grad", final, grad_o)
    sc.pump(rush=True)
    vec[...] = vs.total()
    for s in range(8):
        @pl.when(l.s == s)
        def _():
            for r, o in ((TG, tg_o), (TS, ts_o), (TOB, tob_o), (TLB, tlb_o), (SG, sg_o), (SS, ss_o), (SOB, sob_o), (FG, fg_o),
                         (FS, fs_o), (FRB, frb_o)):
                o[...] = vec[r, 96 * s:96 * s + 96]
            for r, o in ((TIB, tib_o), (SIB, sib_o)):
                o[...] = vec[r + s // 4, 192 * (s % 4):192 * (s % 4) + 192]
            t, lane = FEB + 2 * (s % 2), 192 * (s // 2)
            feb_o[...] = jnp.concatenate([vec[t:t + 1, lane:lane + 192], vec[t + 1:t + 2, lane:lane + 192]], axis=1).reshape(384)
    sc.finish()
    l.drain()
    here.drain()


LIMIT = 63 << 20
VM = pl.BlockSpec(memory_space=pltpu.VMEM)
ANY = pl.BlockSpec(memory_space=pl.ANY)


def hand_over(*refs):
    for i in range(22):
        refs[22 + i][...] = refs[i][...]


def on_device_fast(
    tokens, cotangent, frame_clip, frame_valid, place_valid,
    time_gain, time_shift, time_inward, time_inward_bias, time_outward, time_outward_bias, time_linear, time_linear_bias,
    space_gain, space_shift, space_inward, space_inward_bias, space_outward, space_outward_bias,
    feed_gain, feed_shift, feed_expand, feed_expand_bias, feed_reduce, feed_reduce_bias,
):
    vectors = jnp.concatenate([
        time_gain, time_shift, time_outward_bias, time_linear_bias, space_gain, space_shift, space_outward_bias, feed_gain,
        feed_shift, feed_reduce_bias, time_inward_bias, space_inward_bias, feed_expand_bias])
    vin = jnp.pad(vectors.reshape(18, 96), ((0, 6), (0, 32)))
    shaped, vmem = jax.ShapeDtypeStruct, pltpu.VMEM
    rows_bf, rows_f32 = vmem((1024, 768), BF), vmem((1024, 768), F32)
    by_frame, by_place = vmem((4, 32, 8, 768), BF), vmem((32, 4, 8, 768), BF)
    row_block, selector = vmem((SLOTS, 96, 768), BF), vmem((192, 128), BF)
    n = CHUNKS * 20 + 14 + 28 + 56 + 6
    parameters = (
        time_gain, time_shift, time_inward, time_inward_bias, time_outward, time_outward_bias, time_linear, time_linear_bias,
        space_gain, space_shift, space_inward, space_inward_bias, space_outward, space_outward_bias,
        feed_gain, feed_shift, feed_expand, feed_expand_bias, feed_reduce, feed_reduce_bias)
    outs = pl.pallas_call(
        layer_kernel,
        out_shape=(shaped((1024, 768), BF), shaped((1024, 768), F32)) + tuple(shaped(p.shape, F32) for p in parameters) + (
            shaped((1024, 2304), BF), shaped((1024, 768), BF), shaped((1024, 768), BF), shaped((1024, 768), F32),
            shaped((32, 4, 8, 768), BF)),
        in_specs=[ANY, ANY] + [VM] * 11,
        out_specs=(ANY, ANY) + (VM,) * 20 + (ANY,) * 5,
        scratch_shapes=[
            vmem((WROWS, 768), BF), vmem((4, CHUNKS, 144, 128), BF), vmem((8, 24, 128), F32), vmem((24, 768), F32),
            selector, selector, selector, selector, vmem((256, 256), F32), vmem((4, 256, 1), F32),
            by_frame, by_frame, by_place, by_place, rows_bf, rows_bf, vmem((1024, 2304), BF), rows_f32, rows_f32, rows_f32,
            rows_bf, rows_bf, rows_bf,
            vmem((SLOTS, 4, 96, 768), BF), row_block, row_block, row_block, vmem((SLOTS, 4, 144, 128), BF),
            vmem((SLOTS, 3, 144, 128), BF), vmem((4, 24, 768), F32), vmem((7, 24, 768), F32), vmem((96, 256), F32),
            pltpu.SemaphoreType.DMA((24,)), pltpu.SemaphoreType.DMA((n,)), pltpu.SemaphoreType.DMA((n,))],
        compiler_params=pltpu.CompilerParams(collective_id=0, has_side_effects=True, vmem_limit_bytes=LIMIT),
    )(tokens.reshape(4, 32, 8, 768), cotangent.reshape(1024, 768), frame_clip.reshape(1, 32), frame_valid.reshape(1, 32),
      place_valid, vin, time_inward, time_outward, time_linear, space_inward, space_outward, feed_expand, feed_reduce)
    outs = pl.pallas_call(
        hand_over, out_shape=tuple(shaped(o.shape, o.dtype) for o in outs[:22]), in_specs=[VM] * 22, out_specs=(VM,) * 22,
        compiler_params=pltpu.CompilerParams(vmem_limit_bytes=32 << 20))(*outs[:22])
    return (outs[0].reshape(tokens.shape), outs[1].reshape(tokens.shape)) + tuple(outs[2:])


HEADS = 12


def normalize(inputs, scaling, offset):
    average = jnp.mean(inputs, axis=-1, keepdims=True)
    centered = inputs - average
    variance = jnp.mean(centered * centered, axis=-1, keepdims=True)
    return centered * lax.rsqrt(variance + EPSILON) * scaling + offset


def gelu_exact(inputs):
    return jax.nn.gelu(inputs, approximate=False)


def matmul(former, latter):
    return jnp.dot(former, latter, preferred_element_type=jnp.float32)


def inner(former, latter):
    return lax.dot_general(
        former, latter, (((0,), (0,)), ((), ())), preferred_element_type=jnp.float32
    )


def against(former, latter):
    return lax.dot_general(
        former, latter, (((1,), (1,)), ((), ())), preferred_element_type=jnp.float32
    )


def column_sum(delta_rows):
    return jnp.sum(delta_rows, axis=0, dtype=jnp.float32)


def packed_sum(joined_grad):
    totals = jnp.sum(joined_grad, axis=0, dtype=jnp.float32)
    model_width = totals.shape[0] // 3
    return jnp.concatenate([totals[:model_width], totals[2 * model_width :]])


def patterns(flavor):
    if flavor == "time":
        return ("fphd,gphd->phfg", "phfg,gphd->fphd", "phfg,fphd->gphd")
    return ("fphd,fqhd->fhpq", "fhpq,fqhd->fphd", "fhpq,fphd->fqhd")


def project_in_general(normed_low, weight, packed_bias, leading, head_count):
    model_width = normed_low.shape[-1]
    full_bias = jnp.concatenate(
        [
            packed_bias[:model_width],
            jnp.zeros((model_width,), jnp.float32),
            packed_bias[model_width:],
        ]
    )
    joined = (matmul(normed_low, weight) + full_bias).astype(jnp.bfloat16)
    shaped = joined.reshape(leading + (3, head_count, model_width // head_count))
    return (shaped[:, :, 0], shaped[:, :, 1], shaped[:, :, 2])


def attend(queries, keys_in, values, allowed, flavor):
    score_form, mix_form, spare_form = patterns(flavor)
    factor = queries.shape[-1] ** (-0.5)
    scores = jnp.einsum(score_form, queries, keys_in, preferred_element_type=jnp.float32) * factor
    masked = jnp.where(allowed, scores, -1e30)
    highest = jnp.max(masked, axis=-1, keepdims=True)
    raised = jnp.exp(masked - highest)
    summed = jnp.sum(raised, axis=-1, keepdims=True)
    chances = (raised / summed).astype(jnp.bfloat16)
    mixed = jnp.einsum(mix_form, chances, values, preferred_element_type=jnp.float32)
    return (mixed, highest + jnp.log(summed))


def attend_back(queries, keys_in, values, log_total, allowed, upstream, flavor):
    score_form, mix_form, spare_form = patterns(flavor)
    factor = queries.shape[-1] ** (-0.5)
    scores = jnp.einsum(score_form, queries, keys_in, preferred_element_type=jnp.float32) * factor
    chances = jnp.exp(jnp.where(allowed, scores, -1e30) - log_total)
    value_grad = jnp.einsum(
        spare_form, chances.astype(jnp.bfloat16), upstream, preferred_element_type=jnp.float32
    )
    chance_grad = jnp.einsum(score_form, upstream, values, preferred_element_type=jnp.float32)
    score_grad = (
        chances * (chance_grad - jnp.sum(chance_grad * chances, axis=-1, keepdims=True))
    ).astype(jnp.bfloat16)
    query_grad = (
        jnp.einsum(mix_form, score_grad, keys_in, preferred_element_type=jnp.float32) * factor
    )
    key_grad = (
        jnp.einsum(spare_form, score_grad, queries, preferred_element_type=jnp.float32) * factor
    )
    joined = jnp.stack([query_grad, key_grad, value_grad], axis=2)
    return joined.reshape(-1, 3 * joined.shape[-1] * joined.shape[-2]).astype(jnp.bfloat16)


def on_device_general(
    tokens,
    cotangent,
    frame_clip,
    frame_valid,
    place_valid,
    time_gain,
    time_shift,
    time_inward,
    time_inward_bias,
    time_outward,
    time_outward_bias,
    time_linear,
    time_linear_bias,
    space_gain,
    space_shift,
    space_inward,
    space_inward_bias,
    space_outward,
    space_outward_bias,
    feed_gain,
    feed_shift,
    feed_expand,
    feed_expand_bias,
    feed_reduce,
    feed_reduce_bias,
):
    frames_dev, places, model_width = tokens.shape
    head_count = HEADS
    group_frames = frame_clip.shape[0]
    clip_count = place_valid.shape[0]
    place_dev = places // lax.axis_size("seq")
    rows_part = (
        lax.all_gather(time_inward.astype(jnp.bfloat16), "grp", axis=0, tiled=True),
        lax.all_gather(time_outward.astype(jnp.bfloat16), "grp", axis=0, tiled=True),
        lax.all_gather(time_linear.astype(jnp.bfloat16), "grp", axis=0, tiled=True),
        lax.all_gather(space_inward.astype(jnp.bfloat16), "grp", axis=0, tiled=True),
        lax.all_gather(space_outward.astype(jnp.bfloat16), "grp", axis=0, tiled=True),
        lax.all_gather(feed_expand.astype(jnp.bfloat16), "grp", axis=0, tiled=True),
        lax.all_gather(feed_reduce.astype(jnp.bfloat16), "grp", axis=0, tiled=True),
    )
    gathered = (
        lax.all_gather(rows_part[0], "seq", axis=1, tiled=True),
        lax.all_gather(rows_part[1], "seq", axis=1, tiled=True),
        lax.all_gather(rows_part[2], "seq", axis=1, tiled=True),
        lax.all_gather(rows_part[3], "seq", axis=1, tiled=True),
        lax.all_gather(rows_part[4], "seq", axis=1, tiled=True),
        lax.all_gather(rows_part[5], "seq", axis=1, tiled=True),
        lax.all_gather(rows_part[6], "seq", axis=1, tiled=True),
        lax.all_gather(time_gain.astype(jnp.bfloat16), "seq", axis=0, tiled=True),
        lax.all_gather(time_shift.astype(jnp.bfloat16), "seq", axis=0, tiled=True),
        lax.all_gather(time_inward_bias.astype(jnp.bfloat16), "seq", axis=0, tiled=True),
        lax.all_gather(time_outward_bias.astype(jnp.bfloat16), "seq", axis=0, tiled=True),
        lax.all_gather(time_linear_bias.astype(jnp.bfloat16), "seq", axis=0, tiled=True),
        lax.all_gather(space_gain.astype(jnp.bfloat16), "seq", axis=0, tiled=True),
        lax.all_gather(space_shift.astype(jnp.bfloat16), "seq", axis=0, tiled=True),
        lax.all_gather(space_inward_bias.astype(jnp.bfloat16), "seq", axis=0, tiled=True),
        lax.all_gather(space_outward_bias.astype(jnp.bfloat16), "seq", axis=0, tiled=True),
        lax.all_gather(feed_gain.astype(jnp.bfloat16), "seq", axis=0, tiled=True),
        lax.all_gather(feed_shift.astype(jnp.bfloat16), "seq", axis=0, tiled=True),
        lax.all_gather(feed_expand_bias.astype(jnp.bfloat16), "seq", axis=0, tiled=True),
        lax.all_gather(feed_reduce_bias.astype(jnp.bfloat16), "seq", axis=0, tiled=True),
    )
    own_slot = lax.axis_index("seq")
    own_clips = lax.dynamic_slice_in_dim(frame_clip, own_slot * frames_dev, frames_dev) % clip_count
    matches = own_clips[:, None] == jnp.arange(clip_count, dtype=jnp.int32)[None, :]
    key_places = jnp.sum(jnp.where(matches[:, :, None], place_valid[None, :, :], 0), axis=1)
    space_allowed = (key_places == 1)[:, None, None, :]
    time_allowed = ((frame_clip[:, None] == frame_clip[None, :]) & (frame_valid[None, :] == 1))[
        None, None
    ]
    placed = lax.all_to_all(tokens, "seq", split_axis=1, concat_axis=0, tiled=True)
    placed_rows = placed.reshape(-1, model_width).astype(jnp.float32)
    time_normed_wide, time_norm_pull = jax.vjp(
        normalize,
        placed_rows,
        gathered[7].astype(jnp.float32),
        gathered[8].astype(jnp.float32),
    )
    time_normed = time_normed_wide.astype(jnp.bfloat16)
    time_parts = project_in_general(
        time_normed,
        gathered[0],
        gathered[9].astype(jnp.float32),
        (group_frames, place_dev),
        head_count,
    )
    time_mixed, time_total = attend(
        time_parts[0], time_parts[1], time_parts[2], time_allowed, "time"
    )
    time_mixed_low = time_mixed.reshape(-1, model_width).astype(jnp.bfloat16)
    time_proj = (
        matmul(time_mixed_low, gathered[1]) + gathered[10].astype(jnp.float32)
    ).astype(jnp.bfloat16)
    returned = lax.all_to_all(
        time_proj.reshape(group_frames, place_dev, model_width),
        "seq",
        split_axis=0,
        concat_axis=1,
        tiled=True,
    )
    returned_rows = returned.reshape(-1, model_width)
    first_sum = (
        tokens.reshape(-1, model_width).astype(jnp.float32)
        + matmul(returned_rows, gathered[2])
        + gathered[11].astype(jnp.float32)
    )
    space_normed_wide, space_norm_pull = jax.vjp(
        normalize,
        first_sum,
        gathered[12].astype(jnp.float32),
        gathered[13].astype(jnp.float32),
    )
    space_normed = space_normed_wide.astype(jnp.bfloat16)
    space_parts = project_in_general(
        space_normed,
        gathered[3],
        gathered[14].astype(jnp.float32),
        (frames_dev, places),
        head_count,
    )
    space_mixed, space_total = attend(
        space_parts[0], space_parts[1], space_parts[2], space_allowed, "space"
    )
    space_mixed_low = space_mixed.reshape(-1, model_width).astype(jnp.bfloat16)
    second_sum = (
        first_sum
        + matmul(space_mixed_low, gathered[4])
        + gathered[15].astype(jnp.float32)
    )
    feed_normed_wide, feed_norm_pull = jax.vjp(
        normalize,
        second_sum,
        gathered[16].astype(jnp.float32),
        gathered[17].astype(jnp.float32),
    )
    feed_normed = feed_normed_wide.astype(jnp.bfloat16)
    hidden = matmul(feed_normed, gathered[5]) + gathered[18].astype(jnp.float32)
    activated_wide, gelu_pull = jax.vjp(gelu_exact, hidden)
    activated = activated_wide.astype(jnp.bfloat16)
    final_sum = (
        second_sum
        + matmul(activated, gathered[6])
        + gathered[19].astype(jnp.float32)
    )
    result = final_sum.astype(jnp.bfloat16).reshape(tokens.shape)
    rows_again = (
        lax.all_gather(time_inward.astype(jnp.bfloat16), "grp", axis=0, tiled=True),
        lax.all_gather(time_outward.astype(jnp.bfloat16), "grp", axis=0, tiled=True),
        lax.all_gather(time_linear.astype(jnp.bfloat16), "grp", axis=0, tiled=True),
        lax.all_gather(space_inward.astype(jnp.bfloat16), "grp", axis=0, tiled=True),
        lax.all_gather(space_outward.astype(jnp.bfloat16), "grp", axis=0, tiled=True),
        lax.all_gather(feed_expand.astype(jnp.bfloat16), "grp", axis=0, tiled=True),
        lax.all_gather(feed_reduce.astype(jnp.bfloat16), "grp", axis=0, tiled=True),
    )
    gathered_again = (
        lax.all_gather(rows_again[0], "seq", axis=1, tiled=True),
        lax.all_gather(rows_again[1], "seq", axis=1, tiled=True),
        lax.all_gather(rows_again[2], "seq", axis=1, tiled=True),
        lax.all_gather(rows_again[3], "seq", axis=1, tiled=True),
        lax.all_gather(rows_again[4], "seq", axis=1, tiled=True),
        lax.all_gather(rows_again[5], "seq", axis=1, tiled=True),
        lax.all_gather(rows_again[6], "seq", axis=1, tiled=True),
        lax.all_gather(time_gain.astype(jnp.bfloat16), "seq", axis=0, tiled=True),
        lax.all_gather(time_shift.astype(jnp.bfloat16), "seq", axis=0, tiled=True),
        lax.all_gather(time_inward_bias.astype(jnp.bfloat16), "seq", axis=0, tiled=True),
        lax.all_gather(time_outward_bias.astype(jnp.bfloat16), "seq", axis=0, tiled=True),
        lax.all_gather(time_linear_bias.astype(jnp.bfloat16), "seq", axis=0, tiled=True),
        lax.all_gather(space_gain.astype(jnp.bfloat16), "seq", axis=0, tiled=True),
        lax.all_gather(space_shift.astype(jnp.bfloat16), "seq", axis=0, tiled=True),
        lax.all_gather(space_inward_bias.astype(jnp.bfloat16), "seq", axis=0, tiled=True),
        lax.all_gather(space_outward_bias.astype(jnp.bfloat16), "seq", axis=0, tiled=True),
        lax.all_gather(feed_gain.astype(jnp.bfloat16), "seq", axis=0, tiled=True),
        lax.all_gather(feed_shift.astype(jnp.bfloat16), "seq", axis=0, tiled=True),
        lax.all_gather(feed_expand_bias.astype(jnp.bfloat16), "seq", axis=0, tiled=True),
        lax.all_gather(feed_reduce_bias.astype(jnp.bfloat16), "seq", axis=0, tiled=True),
    )
    upstream = cotangent.reshape(-1, model_width).astype(jnp.float32)
    feed_delta = cotangent.reshape(-1, model_width)
    gradient_feed_reduce = inner(activated, feed_delta)
    gradient_feed_reduce_bias = column_sum(feed_delta)
    (hidden_wide,) = gelu_pull(against(feed_delta, gathered_again[6]))
    hidden_delta = hidden_wide.astype(jnp.bfloat16)
    gradient_feed_expand = inner(feed_normed, hidden_delta)
    gradient_feed_expand_bias = column_sum(hidden_delta)
    second_back, gradient_feed_gain, gradient_feed_shift = feed_norm_pull(
        against(hidden_delta, gathered_again[5])
    )
    second_delta = upstream + second_back
    space_delta = second_delta.astype(jnp.bfloat16)
    gradient_space_outward = inner(space_mixed_low, space_delta)
    gradient_space_outward_bias = column_sum(space_delta)
    space_mixed_delta = against(space_delta, gathered_again[4]).astype(jnp.bfloat16)
    space_mixed_delta = space_mixed_delta.reshape(frames_dev, places, head_count, -1)
    space_joined = attend_back(
        space_parts[0],
        space_parts[1],
        space_parts[2],
        space_total,
        space_allowed,
        space_mixed_delta,
        "space",
    )
    gradient_space_inward = inner(space_normed, space_joined)
    gradient_space_inward_bias = packed_sum(space_joined)
    first_back, gradient_space_gain, gradient_space_shift = space_norm_pull(
        against(space_joined, gathered_again[3])
    )
    first_delta = second_delta + first_back
    linear_delta = first_delta.astype(jnp.bfloat16)
    gradient_time_linear = inner(returned_rows, linear_delta)
    gradient_time_linear_bias = column_sum(linear_delta)
    proj_delta = against(linear_delta, gathered_again[2]).astype(jnp.bfloat16)
    proj_placed = lax.all_to_all(
        proj_delta.reshape(frames_dev, places, model_width),
        "seq",
        split_axis=1,
        concat_axis=0,
        tiled=True,
    )
    proj_rows = proj_placed.reshape(-1, model_width)
    gradient_time_outward = inner(time_mixed_low, proj_rows)
    gradient_time_outward_bias = column_sum(proj_rows)
    time_mixed_delta = against(proj_rows, gathered_again[1]).astype(jnp.bfloat16)
    time_mixed_delta = time_mixed_delta.reshape(group_frames, place_dev, head_count, -1)
    time_joined = attend_back(
        time_parts[0],
        time_parts[1],
        time_parts[2],
        time_total,
        time_allowed,
        time_mixed_delta,
        "time",
    )
    gradient_time_inward = inner(time_normed, time_joined)
    gradient_time_inward_bias = packed_sum(time_joined)
    placed_back, gradient_time_gain, gradient_time_shift = time_norm_pull(
        against(time_joined, gathered_again[0])
    )
    framed_back = lax.all_to_all(
        placed_back.reshape(group_frames, place_dev, model_width).astype(jnp.bfloat16),
        "seq",
        split_axis=0,
        concat_axis=1,
        tiled=True,
    ).astype(jnp.float32)
    input_gradient = (first_delta + framed_back.reshape(-1, model_width)).reshape(tokens.shape)
    matrix_terms = (
        gradient_time_inward,
        gradient_time_outward,
        gradient_time_linear,
        gradient_space_inward,
        gradient_space_outward,
        gradient_feed_expand,
        gradient_feed_reduce,
    )
    vector_terms = (
        gradient_time_gain,
        gradient_time_shift,
        gradient_time_inward_bias,
        gradient_time_outward_bias,
        gradient_time_linear_bias,
        gradient_space_gain,
        gradient_space_shift,
        gradient_space_inward_bias,
        gradient_space_outward_bias,
        gradient_feed_gain,
        gradient_feed_shift,
        gradient_feed_expand_bias,
        gradient_feed_reduce_bias,
    )
    columns_summed = (
        lax.psum_scatter(
            matrix_terms[0].astype(jnp.bfloat16), "seq", scatter_dimension=1, tiled=True
        ).astype(jnp.float32),
        lax.psum_scatter(
            matrix_terms[1].astype(jnp.bfloat16), "seq", scatter_dimension=1, tiled=True
        ).astype(jnp.float32),
        lax.psum_scatter(
            matrix_terms[2].astype(jnp.bfloat16), "seq", scatter_dimension=1, tiled=True
        ).astype(jnp.float32),
        lax.psum_scatter(
            matrix_terms[3].astype(jnp.bfloat16), "seq", scatter_dimension=1, tiled=True
        ).astype(jnp.float32),
        lax.psum_scatter(
            matrix_terms[4].astype(jnp.bfloat16), "seq", scatter_dimension=1, tiled=True
        ).astype(jnp.float32),
        lax.psum_scatter(
            matrix_terms[5].astype(jnp.bfloat16), "seq", scatter_dimension=1, tiled=True
        ).astype(jnp.float32),
        lax.psum_scatter(
            matrix_terms[6].astype(jnp.bfloat16), "seq", scatter_dimension=1, tiled=True
        ).astype(jnp.float32),
        lax.psum_scatter(
            vector_terms[0].astype(jnp.bfloat16), "seq", scatter_dimension=0, tiled=True
        ).astype(jnp.float32),
        lax.psum_scatter(
            vector_terms[1].astype(jnp.bfloat16), "seq", scatter_dimension=0, tiled=True
        ).astype(jnp.float32),
        lax.psum_scatter(
            vector_terms[2].astype(jnp.bfloat16), "seq", scatter_dimension=0, tiled=True
        ).astype(jnp.float32),
        lax.psum_scatter(
            vector_terms[3].astype(jnp.bfloat16), "seq", scatter_dimension=0, tiled=True
        ).astype(jnp.float32),
        lax.psum_scatter(
            vector_terms[4].astype(jnp.bfloat16), "seq", scatter_dimension=0, tiled=True
        ).astype(jnp.float32),
        lax.psum_scatter(
            vector_terms[5].astype(jnp.bfloat16), "seq", scatter_dimension=0, tiled=True
        ).astype(jnp.float32),
        lax.psum_scatter(
            vector_terms[6].astype(jnp.bfloat16), "seq", scatter_dimension=0, tiled=True
        ).astype(jnp.float32),
        lax.psum_scatter(
            vector_terms[7].astype(jnp.bfloat16), "seq", scatter_dimension=0, tiled=True
        ).astype(jnp.float32),
        lax.psum_scatter(
            vector_terms[8].astype(jnp.bfloat16), "seq", scatter_dimension=0, tiled=True
        ).astype(jnp.float32),
        lax.psum_scatter(
            vector_terms[9].astype(jnp.bfloat16), "seq", scatter_dimension=0, tiled=True
        ).astype(jnp.float32),
        lax.psum_scatter(
            vector_terms[10].astype(jnp.bfloat16), "seq", scatter_dimension=0, tiled=True
        ).astype(jnp.float32),
        lax.psum_scatter(
            vector_terms[11].astype(jnp.bfloat16), "seq", scatter_dimension=0, tiled=True
        ).astype(jnp.float32),
        lax.psum_scatter(
            vector_terms[12].astype(jnp.bfloat16), "seq", scatter_dimension=0, tiled=True
        ).astype(jnp.float32),
    )
    rows_summed = (
        lax.psum_scatter(
            columns_summed[0].astype(jnp.bfloat16), "grp", scatter_dimension=0, tiled=True
        ).astype(jnp.float32),
        lax.psum_scatter(
            columns_summed[1].astype(jnp.bfloat16), "grp", scatter_dimension=0, tiled=True
        ).astype(jnp.float32),
        lax.psum_scatter(
            columns_summed[2].astype(jnp.bfloat16), "grp", scatter_dimension=0, tiled=True
        ).astype(jnp.float32),
        lax.psum_scatter(
            columns_summed[3].astype(jnp.bfloat16), "grp", scatter_dimension=0, tiled=True
        ).astype(jnp.float32),
        lax.psum_scatter(
            columns_summed[4].astype(jnp.bfloat16), "grp", scatter_dimension=0, tiled=True
        ).astype(jnp.float32),
        lax.psum_scatter(
            columns_summed[5].astype(jnp.bfloat16), "grp", scatter_dimension=0, tiled=True
        ).astype(jnp.float32),
        lax.psum_scatter(
            columns_summed[6].astype(jnp.bfloat16), "grp", scatter_dimension=0, tiled=True
        ).astype(jnp.float32),
    )
    vector_shares = tuple(columns_summed[7:])
    vectors_summed = lax.psum(
        (
            vector_shares[0],
            vector_shares[1],
            vector_shares[2],
            vector_shares[3],
            vector_shares[4],
            vector_shares[5],
            vector_shares[6],
            vector_shares[7],
            vector_shares[8],
            vector_shares[9],
            vector_shares[10],
            vector_shares[11],
            vector_shares[12],
        ),
        "grp",
    )
    owned = tuple(rows_summed) + tuple(vectors_summed)
    return (result, input_gradient) + tuple(owned[i] for i in (7, 8, 0, 9, 1, 10, 2, 11, 12, 13, 3, 14, 4, 15, 16, 17, 5, 18, 6, 19))


def solution(mesh):
    fast = mesh.shape["grp"] == 4 and mesh.shape["seq"] == 8
    return jax.shard_map(
        on_device_fast if fast else on_device_general,
        mesh=mesh,
        in_specs=(
            P(("grp", "seq"), None, None),
            P(("grp", "seq"), None, None),
            P("grp"),
            P("grp"),
            P("grp", None),
            P("seq"),
            P("seq"),
            P("grp", "seq"),
            P("seq"),
            P("grp", "seq"),
            P("seq"),
            P("grp", "seq"),
            P("seq"),
            P("seq"),
            P("seq"),
            P("grp", "seq"),
            P("seq"),
            P("grp", "seq"),
            P("seq"),
            P("seq"),
            P("seq"),
            P("grp", "seq"),
            P("seq"),
            P("grp", "seq"),
            P("seq"),
        ),
        out_specs=(
            P(("grp", "seq"), None, None),
            P(("grp", "seq"), None, None),
            P("seq"),
            P("seq"),
            P("grp", "seq"),
            P("seq"),
            P("grp", "seq"),
            P("seq"),
            P("grp", "seq"),
            P("seq"),
            P("seq"),
            P("seq"),
            P("grp", "seq"),
            P("seq"),
            P("grp", "seq"),
            P("seq"),
            P("seq"),
            P("seq"),
            P("grp", "seq"),
            P("seq"),
            P("grp", "seq"),
            P("seq"),
        ),
        check_vma=False,
    )
```

profile of v0, /device:TPU:0, one launch (start us, length us, event | category | flops | bytes accessed | tf_op | source)
XLA Modules:
  0.0 336.3 jit_solution(17222766822942127246)
XLA Ops:
  0.7 0.9 concatenate.3
  1.6 0.1 reshape.69
  1.6 0.6 pad.4.vin
  2.3 1.9 copy.47.fr_i
  4.1 309.7 %shard_map.408 = (bf16[1024,768]{1,0:T(8,128)(2,1)}, f32[1024,768]{1,0:T(8,128)}, f32[96]{0:T(128)}, f32[96]{0:T(128)}, f32[192,288]{1,0:T(8,128)}, /*index=5*/f...) custom-call(bf16[4,32,8,768]{3,2,1,0:T(8,128)(2,1)} %bitcast.6, ...), custom_call_target="tpu_custom_call" | custom-call | tf_op jit(solution)/shard_map/pallas_call | solution.py:787
  313.8 0.0 copy-start
  313.9 1.9 copy-done
  315.7 0.0 copy-start.1
  315.7 1.4 copy-done.1
  317.1 0.0 copy-start.2
  317.1 1.0 copy-done.2
  318.1 0.0 copy-start.3
  318.1 1.0 copy-done.3
  319.1 0.0 copy-start.4
  319.1 1.0 copy-done.4
  320.1 0.0 copy-start.5
  320.1 1.0 copy-done.5
  321.0 0.0 copy-start.6
  321.0 0.9 copy-done.6
  321.9 0.0 copy-start.7
  321.9 0.9 copy-done.7
  322.8 0.0 copy-start.8
  322.8 0.9 copy-done.8
  323.7 0.0 copy-start.9
  323.7 0.7 copy-done.9
  324.4 0.0 copy-start.10
  324.4 0.7 copy-done.10
  325.1 0.0 copy-start.11
  325.1 0.6 copy-done.11
  325.7 0.0 copy-start.12
  325.7 0.6 copy-done.12
  326.3 0.0 copy-start.13
  326.3 0.6 copy-done.13
  326.9 0.0 copy-start.14
  326.9 0.6 copy-done.14
  327.5 0.0 copy-start.15
  327.5 0.7 copy-done.15
  328.2 0.0 copy-start.16
  328.2 0.6 copy-done.16
  328.8 0.0 copy-start.17
  328.8 0.7 copy-done.17
  329.5 0.0 copy-start.18
  329.5 0.6 copy-done.18
  330.1 0.0 copy-start.19
  330.1 0.7 copy-done.19
  330.7 0.0 copy-start.20
  330.7 0.6 copy-done.20
  331.3 0.0 copy-start.21
  331.3 0.7 copy-done.21
  332.0 2.9 shard_map.409
  335.0 0.9 copy.48
Async XLA Ops:
  313.8 1.9 copy-start
  315.7 1.4 copy-start.1
  317.1 1.0 copy-start.2
  318.1 1.0 copy-start.3
  319.1 1.0 copy-start.4
  320.1 1.0 copy-start.5
  321.0 0.9 copy-start.6
  321.9 0.9 copy-start.7
  322.8 0.9 copy-start.8
  323.7 0.7 copy-start.9
  324.4 0.7 copy-start.10
  325.1 0.6 copy-start.11
  325.7 0.6 copy-start.12
  326.3 0.6 copy-start.13
  326.9 0.6 copy-start.14
  327.5 0.7 copy-start.15
  328.2 0.6 copy-start.16
  328.8 0.7 copy-start.17
  329.5 0.6 copy-start.18
  330.1 0.7 copy-start.19
  330.7 0.6 copy-start.20
  331.3 0.7 copy-start.21
where the time goes:
time: 342 us; the launch traced here: 336 us
  Pallas kernels  313 us (92%)
  local copies, waits for them, and re-layouts  22.5 us (7%)
    pallas_call x1, Pallas kernels, on_device_fast(): pl.pallas_call(layer_kernel, out_shape=(shaped((1024, 768), BF), shaped((...  310 us
    unnamed x46, local copies, waits for them, and re-layouts  20.9 us

commit v1 on v0

--- a/solution.py
+++ b/solution.py
@@ -21,8 +21,8 @@
 CHUNKS = 17
 GATHER_ORDER = [0, 1, 2, 3, 4, 5, 6, 7, 8, 9, 10, 13, 15, 11, 12, 14, 16]
 SLOTS = 5
-LAGS = (1, 2, 2, 2)
-GATHER_LAGS = (1, 2, 1)
+LAGS = (2, 3, 3, 3)
+GATHER_LAGS = (2, 3, 2)
 SPACING = 2
 KINDS = ("p", "q", "so", "d", "sp", "sq", "sd")
 EPSILON = 1e-06
@@ -201,9 +201,9 @@
 
 
 class Scatter:
-    def __init__(self, links, g, sr, fr, ar, br, zp, zr, write):
-        self.l, self.g, self.sr, self.fr, self.ar, self.br = links, g, sr, fr, ar, br
-        self.zp, self.zr, self.write = zp, zr, write
+    def __init__(self, links, local, g, sr, fr, ar, br, zp, zr, ob, out):
+        self.l, self.local, self.g, self.sr, self.fr, self.ar, self.br = links, local, g, sr, fr, ar, br
+        self.zp, self.zr, self.ob, self.out = zp, zr, ob, out
         self.ready, self.flight, self.order = [], [], []
         self.clock, self.pushed = 0, -9
 
@@ -258,7 +258,10 @@
         total = self.zp[k, l.z].astype(F32)
         for j in range(3):
             total += self.zr[k, j].astype(F32)
-        self.write(c, total)
+        if i >= SLOTS:
+            self.local.wait(("o", self.order[i - SLOTS]))
+        self.ob[k] = total
+        self.local.start(("o", c), self.ob.at[k], self.out.at[c])
 
     def pump(self, rush=False):
         steps = (self.step_b, self.step_c, self.step_d, self.step_e)
@@ -325,7 +328,7 @@
             vec[FEB + t:FEB + 1 + t, lane:lane + 96] = piece[FEB + a:FEB + 1 + a, 0:96]
 
 
-def selectors(odd, ea, el, eh, eb):
+def selectors(odd, ea, el, eh):
     m = lax.broadcasted_iota(jnp.int32, (192, 128), 0)
     c = lax.broadcasted_iota(jnp.int32, (192, 128), 1)
     whole, folded = c + 64 * odd, c % 64 + 128 * (1 - odd)
@@ -333,7 +336,6 @@
     both = jnp.where(m == folded, 1.0, 0.0)
     el[...] = jnp.where(c < 64, both, 0.0).astype(BF)
     eh[...] = jnp.where(c < 64, 0.0, both).astype(BF)
-    eb[...] = both.astype(BF)
 
 
 def standardize(x):
@@ -440,10 +442,9 @@
 
 def layer_kernel(
     tokens, cot_i, clip_i, valid_i, place_i, vin, ti_i, to_i, tl_i, si_i, so_i, fe_i, fr_i,
-    result_o, grad_o, tg_o, ts_o, gti, tib_o, gto, tob_o, gtl, tlb_o, sg_o, ss_o, gsi, sib_o, gso, sob_o, fg_o, fs_o, gfe, feb_o,
-    gfr, frb_o, tqkv_o, tmixed_o, ret_o, first_o, xp_o,
-    w, zst, vg, vec, ea, el, eh, eb, tmask, smask, frames_a, frames_b, places_a, places_b, nb, mixed, qkv, f1, f2, f3, act, gh, g,
-    sr, fr, ar, br, zp, zr, gv, vb, lse, local_sem, send_sem, recv_sem,
+    result_o, grad_o, packed_o, total_o, tqkv_o, tmixed_o, ret_o, first_o, xp_o,
+    w, zst, vg, vec, ea, el, eh, tmask, smask, frames_a, frames_b, places_a, places_b, nb, mixed, qkv, f1, f2, f3, act, gh, g,
+    sr, fr, ar, br, zp, zr, ob, gv, vb, lse, local_sem, send_sem, recv_sem,
 ):
     l = Links(send_sem, recv_sem)
     l.greet()
@@ -457,7 +458,7 @@
     here.start("xp", tokens.at[:, mine], xp.at[mine])
     here.start("cot", cot_i, g)
     odd = l.z % 2
-    selectors(odd, ea, el, eh, eb)
+    selectors(odd, ea, el, eh)
     ga = Gather(l, zst, w)
 
     def pack(ref, chunks):
@@ -505,7 +506,9 @@
     ga.tick()
     ga.zsend(2)
     for t in range(4):
-        pack(fr_i.at[192 * t:192 * t + 192], [13 + t])
+        low = fr_i[:, 192 * t:192 * t + 192].astype(BF)
+        zst[l.z, 13 + t, 0:96] = dot(low, ea[...], NN).astype(BF)
+        zst[l.z, 13 + t, 96:144] = (dot(low[:48], el[...], NN) + dot(low[48:], eh[...], NN)).astype(BF)
     ga.tick()
     masks()
     l.got(*[("v", k) for k in range(1, 8)])
@@ -571,22 +574,7 @@
         final[rows, :] = value + vec[FRB:FRB + 1, :]
         dfn[rows, :] = jnp.zeros((256, 768), F32)
 
-    into = {0: gti, 1: gti, 2: gti, 3: gto, 4: gtl, 5: gsi, 6: gsi, 7: gsi, 8: gso, 9: gfe, 10: gfe, 11: gfe, 12: gfe}
-
-    def write(c, total):
-        a, folded = total[:96], total[96:]
-        lane = lax.broadcasted_iota(jnp.int32, (48, 128), 1)
-        b = jnp.concatenate([jnp.where(lane < 64, folded, 0.0), jnp.where(lane < 64, 0.0, folded)], axis=0)
-        a_high, b_high = a.astype(BF), b.astype(BF)
-        a_low, b_low = (a - a_high.astype(F32)).astype(BF), (b - b_high.astype(F32)).astype(BF)
-        value = (dot(ea[...], a_high, NT) + dot(eb[...], b_high, NT)) + (dot(ea[...], a_low, NT) + dot(eb[...], b_low, NT))
-        if c >= 13:
-            gfr[192 * (c - 13):192 * (c - 12), :] = value
-        else:
-            t = c - [k for k in into if into[k] is into[c]][0]
-            into[c][:, 96 * t:96 * t + 96] = value
-
-    sc = Scatter(l, w, sr, fr, ar, br, zp, zr, write)
+    sc = Scatter(l, here, w, sr, fr, ar, br, zp, zr, ob, packed_o)
     vs = VectorSum(l, gv, vb)
     sums = gv.at[0]
     sums[...] = jnp.zeros((24, 768), F32)
@@ -739,9 +727,45 @@
         final[rows, :] += flat(it[f])
     here.start("grad", final, grad_o)
     sc.pump(rush=True)
-    vec[...] = vs.total()
+    total_o[...] = vs.total()
+    sc.finish()
+    l.drain()
+    here.drain()
+
+
+LIMIT = 63 << 20
+VM = pl.BlockSpec(memory_space=pltpu.VMEM)
+ANY = pl.BlockSpec(memory_space=pl.ANY)
+
+
+def hand_over(
+    result_i, grad_i, packed, vec,
+    result_o, grad_o, tg_o, ts_o, gti, tib_o, gto, tob_o, gtl, tlb_o, sg_o, ss_o, gsi, sib_o, gso, sob_o, fg_o, fs_o, gfe, feb_o,
+    gfr, frb_o, ea, el, eh,
+):
+    selectors(lax.axis_index("grp") % 2, ea, el, eh)
+    result_o[...] = result_i[...]
+    grad_o[...] = grad_i[...]
+    for c in range(CHUNKS):
+        total = packed[c]
+        a, folded = total[:96], total[96:]
+        lane = lax.broadcasted_iota(jnp.int32, (48, 128), 1)
+        b = jnp.concatenate([jnp.where(lane < 64, folded, 0.0), jnp.where(lane < 64, 0.0, folded)], axis=0)
+        eb = el[...] + eh[...]
+        a_high, b_high = a.astype(BF), b.astype(BF)
+        parts = ((ea[...], a_high), (eb, b_high), (ea[...], (a - a_high.astype(F32)).astype(BF)),
+                 (eb, (b - b_high.astype(F32)).astype(BF)))
+        if c >= 13:
+            value = sum(dot(half, e, NT) for e, half in parts)
+            gfr[:, 192 * (c - 13):192 * (c - 12)] = value
+        else:
+            value = sum(dot(e, half, NT) for e, half in parts)
+            out = (gti, gti, gti, gto, gtl, gsi, gsi, gsi, gso, gfe, gfe, gfe, gfe)[c]
+            t = (0, 1, 2, 0, 0, 0, 1, 2, 0, 0, 1, 2, 3)[c]
+            out[:, 96 * t:96 * t + 96] = value
+    me = lax.axis_index("seq")
     for s in range(8):
-        @pl.when(l.s == s)
+        @pl.when(me == s)
         def _():
             for r, o in ((TG, tg_o), (TS, ts_o), (TOB, tob_o), (TLB, tlb_o), (SG, sg_o), (SS, ss_o), (SOB, sob_o), (FG, fg_o),
                          (FS, fs_o), (FRB, frb_o)):
@@ -750,19 +774,6 @@
                 o[...] = vec[r + s // 4, 192 * (s % 4):192 * (s % 4) + 192]
             t, lane = FEB + 2 * (s % 2), 192 * (s // 2)
             feb_o[...] = jnp.concatenate([vec[t:t + 1, lane:lane + 192], vec[t + 1:t + 2, lane:lane + 192]], axis=1).reshape(384)
-    sc.finish()
-    l.drain()
-    here.drain()
-
-
-LIMIT = 63 << 20
-VM = pl.BlockSpec(memory_space=pltpu.VMEM)
-ANY = pl.BlockSpec(memory_space=pl.ANY)
-
-
-def hand_over(*refs):
-    for i in range(22):
-        refs[22 + i][...] = refs[i][...]
 
 
 def on_device_fast(
@@ -786,25 +797,30 @@
         feed_gain, feed_shift, feed_expand, feed_expand_bias, feed_reduce, feed_reduce_bias)
     outs = pl.pallas_call(
         layer_kernel,
-        out_shape=(shaped((1024, 768), BF), shaped((1024, 768), F32)) + tuple(shaped(p.shape, F32) for p in parameters) + (
+        out_shape=(
+            shaped((1024, 768), BF), shaped((1024, 768), F32), shaped((CHUNKS, 144, 128), F32), shaped((24, 768), F32),
             shaped((1024, 2304), BF), shaped((1024, 768), BF), shaped((1024, 768), BF), shaped((1024, 768), F32),
             shaped((32, 4, 8, 768), BF)),
         in_specs=[ANY, ANY] + [VM] * 11,
-        out_specs=(ANY, ANY) + (VM,) * 20 + (ANY,) * 5,
+        out_specs=(ANY, ANY, ANY, VM) + (ANY,) * 5,
         scratch_shapes=[
             vmem((WROWS, 768), BF), vmem((4, CHUNKS, 144, 128), BF), vmem((8, 24, 128), F32), vmem((24, 768), F32),
-            selector, selector, selector, selector, vmem((256, 256), F32), vmem((4, 256, 1), F32),
+            selector, selector, selector, vmem((256, 256), F32), vmem((4, 256, 1), F32),
             by_frame, by_frame, by_place, by_place, rows_bf, rows_bf, vmem((1024, 2304), BF), rows_f32, rows_f32, rows_f32,
             rows_bf, rows_bf, rows_bf,
             vmem((SLOTS, 4, 96, 768), BF), row_block, row_block, row_block, vmem((SLOTS, 4, 144, 128), BF),
-            vmem((SLOTS, 3, 144, 128), BF), vmem((4, 24, 768), F32), vmem((7, 24, 768), F32), vmem((96, 256), F32),
-            pltpu.SemaphoreType.DMA((24,)), pltpu.SemaphoreType.DMA((n,)), pltpu.SemaphoreType.DMA((n,))],
+            vmem((SLOTS, 3, 144, 128), BF), vmem((SLOTS, 144, 128), F32), vmem((4, 24, 768), F32), vmem((7, 24, 768), F32), vmem((96, 256), F32),
+            pltpu.SemaphoreType.DMA((44,)), pltpu.SemaphoreType.DMA((n,)), pltpu.SemaphoreType.DMA((n,))],
         compiler_params=pltpu.CompilerParams(collective_id=0, has_side_effects=True, vmem_limit_bytes=LIMIT),
     )(tokens.reshape(4, 32, 8, 768), cotangent.reshape(1024, 768), frame_clip.reshape(1, 32), frame_valid.reshape(1, 32),
-      place_valid, vin, time_inward, time_outward, time_linear, space_inward, space_outward, feed_expand, feed_reduce)
-    outs = pl.pallas_call(
-        hand_over, out_shape=tuple(shaped(o.shape, o.dtype) for o in outs[:22]), in_specs=[VM] * 22, out_specs=(VM,) * 22,
-        compiler_params=pltpu.CompilerParams(vmem_limit_bytes=32 << 20))(*outs[:22])
+      place_valid, vin, time_inward, time_outward, time_linear, space_inward, space_outward, feed_expand, feed_reduce.T)
+    shapes = [shaped(p.shape, F32) for p in parameters]
+    shapes[18] = shaped(feed_reduce.T.shape, F32)
+    outs = list(pl.pallas_call(
+        hand_over, out_shape=(shaped((1024, 768), BF), shaped((1024, 768), F32)) + tuple(shapes),
+        in_specs=[VM] * 4, out_specs=(VM,) * 22, scratch_shapes=[selector] * 3,
+        compiler_params=pltpu.CompilerParams(vmem_limit_bytes=32 << 20))(*outs[:4]))
+    outs[20] = outs[20].T
     return (outs[0].reshape(tokens.shape), outs[1].reshape(tokens.shape)) + tuple(outs[2:])
 
 

time: 342 us -> 318 us (0.930)
  local copies, waits for them, and re-layouts: 22.5 us -> 7.06 us
  Pallas kernels: 313 us -> 304 us
    unnamed x46 -> x8, local copies, waits for them, and re-layouts: 20.9 us -> 5.47 us
    pallas_call x1, Pallas kernels: 310 us -> 300 us  [on_device_fast(): pl.pallas_call(layer_kernel, out_shape=(shaped((1024, 768), BF), shaped((...]
where the time goes in v1:
time: 318 us; the launch traced here: 312 us
  Pallas kernels  304 us (96%)
  local copies, waits for them, and re-layouts  7.06 us (2%)
    pallas_call x1, Pallas kernels, on_device_fast(): pl.pallas_call(layer_kernel, out_shape=(shaped((1024, 768), BF), shaped((...  300 us

profile of v1, /device:TPU:0, one launch (start us, length us, event | category | flops | bytes accessed | tf_op | source)
XLA Modules:
  0.0 312.4 jit_solution(13980844509593611349)
XLA Ops:
  0.7 0.9 concatenate.3
  1.6 0.1 reshape.69
  1.6 0.6 pad.4.vin
  2.3 299.8 %shard_map.408 = (bf16[1024,768]{1,0:T(8,128)(2,1)}, f32[1024,768]{1,0:T(8,128)}, f32[17,144,128]{2,1,0:T(8,128)}, f32[24,768]{1,0:T(8,128)}, bf16[1024,2304]{1,...) custom-call(bf16[4,32,8,768]{3,2,1,0:T(8,128)(2,1)} %bitcast.8, ...), custom_call_target="tpu_custom_call" | custom-call | tf_op jit(solution)/shard_map/pallas_call | solution.py:798
  302.1 0.0 copy-start
  302.1 1.9 copy-done
  304.0 0.0 copy-start.1
  304.0 1.4 copy-done.1
  305.4 0.0 copy-start.2
  305.4 1.3 copy-done.2
  306.7 0.0 copy-start.3
  306.7 0.9 copy-done.3
  307.6 4.4 %shard_map.409 = (bf16[1024,768]{1,0:T(8,128)(2,1)}, f32[1024,768]{1,0:T(8,128)}, f32[96]{0:T(128)}, f32[96]{0:T(128)}, f32[192,288]{1,0:T(8,128)}, /*index=5*/f...) custom-call(bf16[1024,768]{1,0:T(8,128)(2,1)S(1)} %copy-done.1, ...), custom_call_target="tpu_custom_call" | custom-call | tf_op jit(solution)/shard_map/pallas_call | solution.py:819
Async XLA Ops:
  302.1 1.9 copy-start
  304.0 1.4 copy-start.1
  305.4 1.3 copy-start.2
  306.7 0.9 copy-start.3

commit v2 on v1

--- a/solution.py
+++ b/solution.py
@@ -21,9 +21,10 @@
 CHUNKS = 17
 GATHER_ORDER = [0, 1, 2, 3, 4, 5, 6, 7, 8, 9, 10, 13, 15, 11, 12, 14, 16]
 SLOTS = 5
+EARLY_SLOTS = 8
 LAGS = (2, 3, 3, 3)
-GATHER_LAGS = (2, 3, 2)
-SPACING = 2
+GATHER_LAGS = (3, 5, 3)
+SPACING = 1
 KINDS = ("p", "q", "so", "d", "sp", "sq", "sd")
 EPSILON = 1e-06
 
@@ -224,7 +225,7 @@
             if s is l.d:
                 l.sends(("f", c), block(self.g, c, l.d), self.fr.at[k], l.p)
             if s is l.p:
-                l.sends(("a", c), block(self.g, c, l.p), self.ar.at[k], l.p)
+                l.sends(("a", c), block(self.g, c, l.p), self.ar.at[i % EARLY_SLOTS], l.p)
 
     def step_c(self, i, c):
         l, k = self.l, i % SLOTS
@@ -236,7 +237,7 @@
         l, k = self.l, i % SLOTS
         l.got(("a", c), ("b", c))
         rows = place(c, l.s)
-        total = self.g[rows, :].astype(F32) + self.ar[k].astype(F32) + self.br[k].astype(F32)
+        total = self.g[rows, :].astype(F32) + self.ar[i % EARLY_SLOTS].astype(F32) + self.br[k].astype(F32)
         if i >= SLOTS:
             l.gone(*[("z", self.order[i - SLOTS], j) for j in range(1, 4)])
         zp = self.zp
@@ -636,20 +637,20 @@
         act[rows, :] = low
         note(SOB, column_sums(low.astype(F32)))
         gh[rows, :] = dot(low, w[SO:SO + 768, :], NN).astype(BF)
-        if f % 2:
-            sc.pump(rush=True)
+        sc.pump()
     here.start("result", nb, result_o)
     here.start("first", first_o, first)
     weight_gradient(w.at[SO:SO + 768], act, 0, mixed)
     here.start("mixed2", tmixed_o, mixed)
     sc.ready.append(8)
-    sc.pump(rush=True)
+    sc.pump()
     l.gone(*[("r", b, k) for b in range(4) for k in range(1, 8)])
     here.start("xp2", xp_o, places_b)
     here.wait("result", "first")
     for f in range(4):
         rows = pl.ds(256 * f, 256)
         attend_block_back(f, qkv, gh, lse.at[48:96], lambda: smask[f])
+        sc.pump()
         n, scale = standardize(first[rows, :])
         nb[rows, :] = (n * vec[SG:SG + 1, :] + vec[SS:SS + 1, :]).astype(BF)
         joined = qkv[rows, :]
@@ -668,17 +669,18 @@
         for k in range(1, 8):
             peer = l.speer(k)
             l.sends(("g", f, k), gp.at[f, pl.ds(4 * peer, 4)], gpp.at[4 * l.s + f], peer)
-        sc.pump(rush=True)
+        sc.pump()
     here.start("ret", ret_o, gh)
     for j in range(3):
         weight_gradient(w.at[SI + 768 * j:SI + 768 * (j + 1)], qkv, 768 * j, nb)
+        sc.pump()
     here.start("qkv2", tqkv_o, qkv)
     sc.ready += [5, 6, 7]
-    sc.pump(rush=True)
+    sc.pump()
     here.wait("ret")
     weight_gradient(w.at[TL:TL + 768], act, 0, gh)
     sc.ready.append(4)
-    sc.pump(rush=True)
+    sc.pump()
 
     for f in range(4):
         l.got(*[("g", f, k) for k in range(1, 8)])
@@ -689,15 +691,18 @@
         low = low.astype(BF)
         act[rows, :] = low
         gh[rows, :] = dot(low, w[TO:TO + 768, :], NN).astype(BF)
-    sc.pump(rush=True)
+        if b == 1:
+            sc.pump()
+    sc.pump()
     here.wait("mixed2")
     weight_gradient(w.at[TO:TO + 768], act, 0, mixed)
     sc.ready.append(3)
-    sc.pump(rush=True)
+    sc.pump()
     here.wait("qkv2", "xp2")
     for b in range(4):
         rows = pl.ds(256 * b, 256)
         attend_block_back(b, qkv, gh, lse.at[0:48], lambda: tmask[...])
+        sc.pump()
         n, scale = standardize(flat(places_b[:, b]))
         nb[rows, :] = (n * vec[TG:TG + 1, :] + vec[TS:TS + 1, :]).astype(BF)
         joined = qkv[rows, :]
@@ -711,9 +716,10 @@
         for k in range(1, 8):
             peer = l.speer(k)
             l.sends(("h", b, k), gb.at[pl.ds(4 * peer, 4), b], it.at[:, 4 * l.s + b], peer)
-        sc.pump(rush=True)
+        sc.pump()
     for j in range(3):
         weight_gradient(w.at[TI + 768 * j:TI + 768 * (j + 1)], qkv, 768 * j, nb)
+        sc.pump()
     sc.ready += [0, 1, 2]
     for i in range(3):
         vs.swap(i)
@@ -808,7 +814,7 @@
             selector, selector, selector, vmem((256, 256), F32), vmem((4, 256, 1), F32),
             by_frame, by_frame, by_place, by_place, rows_bf, rows_bf, vmem((1024, 2304), BF), rows_f32, rows_f32, rows_f32,
             rows_bf, rows_bf, rows_bf,
-            vmem((SLOTS, 4, 96, 768), BF), row_block, row_block, row_block, vmem((SLOTS, 4, 144, 128), BF),
+            vmem((SLOTS, 4, 96, 768), BF), row_block, vmem((EARLY_SLOTS, 96, 768), BF), row_block, vmem((SLOTS, 4, 144, 128), BF),
             vmem((SLOTS, 3, 144, 128), BF), vmem((SLOTS, 144, 128), F32), vmem((4, 24, 768), F32), vmem((7, 24, 768), F32), vmem((96, 256), F32),
             pltpu.SemaphoreType.DMA((44,)), pltpu.SemaphoreType.DMA((n,)), pltpu.SemaphoreType.DMA((n,))],
         compiler_params=pltpu.CompilerParams(collective_id=0, has_side_effects=True, vmem_limit_bytes=LIMIT),

time: 318 us -> 310 us (0.975)
  Pallas kernels: 304 us -> 297 us
    pallas_call x1, Pallas kernels: 300 us -> 292 us  [on_device_fast(): pl.pallas_call(layer_kernel, out_shape=(shaped((1024, 768), BF), shaped((...]
where the time goes in v2:
time: 310 us; the launch traced here: 305 us
  Pallas kernels  297 us (96%)
  local copies, waits for them, and re-layouts  7.06 us (2%)
    pallas_call x1, Pallas kernels, on_device_fast(): pl.pallas_call(layer_kernel, out_shape=(shaped((1024, 768), BF), shaped((...  292 us

profile of v2, /device:TPU:0, one launch (start us, length us, event | category | flops | bytes accessed | tf_op | source)
XLA Modules:
  0.0 304.8 jit_solution(9123875468071022315)
XLA Ops:
  0.7 0.9 concatenate.3
  1.6 0.1 reshape.69
  1.6 0.6 pad.4.vin
  2.3 292.1 %shard_map.408 = (bf16[1024,768]{1,0:T(8,128)(2,1)}, f32[1024,768]{1,0:T(8,128)}, f32[17,144,128]{2,1,0:T(8,128)}, f32[24,768]{1,0:T(8,128)}, bf16[1024,2304]{1,...) custom-call(bf16[4,32,8,768]{3,2,1,0:T(8,128)(2,1)} %bitcast.8, ...), custom_call_target="tpu_custom_call" | custom-call | tf_op jit(solution)/shard_map/pallas_call | solution.py:804
  294.4 0.0 copy-start
  294.4 1.9 copy-done
  296.3 0.0 copy-start.1
  296.3 1.4 copy-done.1
  297.7 0.0 copy-start.2
  297.7 1.3 copy-done.2
  299.0 0.0 copy-start.3
  299.0 0.9 copy-done.3
  299.9 4.4 %shard_map.409 = (bf16[1024,768]{1,0:T(8,128)(2,1)}, f32[1024,768]{1,0:T(8,128)}, f32[96]{0:T(128)}, f32[96]{0:T(128)}, f32[192,288]{1,0:T(8,128)}, /*index=5*/f...) custom-call(bf16[1024,768]{1,0:T(8,128)(2,1)S(1)} %copy-done.1, ...), custom_call_target="tpu_custom_call" | custom-call | tf_op jit(solution)/shard_map/pallas_call | solution.py:825
Async XLA Ops:
  294.4 1.9 copy-start
  296.3 1.4 copy-start.1
  297.7 1.3 copy-start.2
  299.0 0.9 copy-start.3

commit v3 on v2

--- a/solution.py
+++ b/solution.py
@@ -745,13 +745,16 @@
 
 
 def hand_over(
-    result_i, grad_i, packed, vec,
+    result_i, grad_i, packed_i, vec_i,
     result_o, grad_o, tg_o, ts_o, gti, tib_o, gto, tob_o, gtl, tlb_o, sg_o, ss_o, gsi, sib_o, gso, sob_o, fg_o, fs_o, gfe, feb_o,
-    gfr, frb_o, ea, el, eh,
+    gfr, frb_o, ea, el, eh, packed, vec, sem,
 ):
+    pairs = ((packed_i, packed), (vec_i, vec), (result_i, result_o), (grad_i, grad_o))
+    copies = [pltpu.make_async_copy(src, dst, sem.at[i]) for i, (src, dst) in enumerate(pairs)]
+    for copy in copies:
+        copy.start()
     selectors(lax.axis_index("grp") % 2, ea, el, eh)
-    result_o[...] = result_i[...]
-    grad_o[...] = grad_i[...]
+    copies[0].wait()
     for c in range(CHUNKS):
         total = packed[c]
         a, folded = total[:96], total[96:]
@@ -770,6 +773,8 @@
             t = (0, 1, 2, 0, 0, 0, 1, 2, 0, 0, 1, 2, 3)[c]
             out[:, 96 * t:96 * t + 96] = value
     me = lax.axis_index("seq")
+    for copy in copies[1:]:
+        copy.wait()
     for s in range(8):
         @pl.when(me == s)
         def _():
@@ -824,7 +829,8 @@
     shapes[18] = shaped(feed_reduce.T.shape, F32)
     outs = list(pl.pallas_call(
         hand_over, out_shape=(shaped((1024, 768), BF), shaped((1024, 768), F32)) + tuple(shapes),
-        in_specs=[VM] * 4, out_specs=(VM,) * 22, scratch_shapes=[selector] * 3,
+        in_specs=[ANY] * 4, out_specs=(VM,) * 22,
+        scratch_shapes=[selector] * 3 + [vmem((CHUNKS, 144, 128), F32), vmem((24, 768), F32), pltpu.SemaphoreType.DMA((4,))],
         compiler_params=pltpu.CompilerParams(vmem_limit_bytes=32 << 20))(*outs[:4]))
     outs[20] = outs[20].T
     return (outs[0].reshape(tokens.shape), outs[1].reshape(tokens.shape)) + tuple(outs[2:])

time: 310 us -> 311 us (level)
  no operation moved by 1% of the time
where the time goes in v3:
time: 311 us; the launch traced here: 305 us
  Pallas kernels  297 us (95%)
  local copies, waits for them, and re-layouts  7.06 us (2%)
    pallas_call x1, Pallas kernels, on_device_fast(): pl.pallas_call(layer_kernel, out_shape=(shaped((1024, 768), BF), shaped((...  292 us

profile of v3, /device:TPU:0, one launch (start us, length us, event | category | flops | bytes accessed | tf_op | source)
XLA Modules:
  0.0 305.4 jit_solution(13198063756796823796)
XLA Ops:
  0.7 0.9 concatenate.3
  1.6 0.1 reshape.69
  1.6 0.6 pad.4.vin
  2.3 292.1 %shard_map.408 = (bf16[1024,768]{1,0:T(8,128)(2,1)}, f32[1024,768]{1,0:T(8,128)}, f32[17,144,128]{2,1,0:T(8,128)}, f32[24,768]{1,0:T(8,128)}, bf16[1024,2304]{1,...) custom-call(bf16[4,32,8,768]{3,2,1,0:T(8,128)(2,1)} %bitcast.8, ...), custom_call_target="tpu_custom_call" | custom-call | tf_op jit(solution)/shard_map/pallas_call | solution.py:809
  294.4 0.0 copy-start
  294.4 1.9 copy-done
  296.3 0.0 copy-start.1
  296.3 1.4 copy-done.1
  297.7 0.0 copy-start.2
  297.7 1.3 copy-done.2
  299.0 0.0 copy-start.3
  299.0 0.9 copy-done.3
  299.9 5.0 %shard_map.409 = (bf16[1024,768]{1,0:T(8,128)(2,1)}, f32[1024,768]{1,0:T(8,128)}, f32[96]{0:T(128)}, f32[96]{0:T(128)}, f32[192,288]{1,0:T(8,128)}, /*index=5*/f...) custom-call(bf16[1024,768]{1,0:T(8,128)(2,1)S(1)} %copy-done.1, ...), custom_call_target="tpu_custom_call" | custom-call | tf_op jit(solution)/shard_map/pallas_call | solution.py:830
Async XLA Ops:
  294.4 1.9 copy-start
  296.3 1.4 copy-start.1
  297.7 1.3 copy-start.2
  299.0 0.9 copy-start.3
